TPU v7x, 32 devices: a whole 2x2x4 slice. The times are simulated.
32 devices in a mesh: gx: 4 (over y, x), gy: 2 (over core), gz: 4 (over z).
Axes of the slice: x: 2, y: 2, z: 4, core: 2. Of those that a mesh axis runs over, the one named last changes fastest.
Arguments:
- positions: float32 [3, 16, 8, 8, 128], P(None, 'gx', 'gy', 'gz'), may hold values from 0 to 128, as said below
- grain_radii: float32 [16, 8, 8, 128], P('gx', 'gy', 'gz'), may hold values from 0.4 to 0.6
- film_liquid: float32 [16, 8, 8, 128], P('gx', 'gy', 'gz'), may hold values from 0.5 to 2
- pair_live: int32 [4, 2, 4, 864], P('gx', 'gy', 'gz'), may hold values from 0 to 1, as said below
- partner: int32 [4, 2, 4, 864, 128], P('gx', 'gy', 'gz'), may hold values from 0 to 127, as said below
- rupture: int32 [4, 2, 4, 864, 128], P('gx', 'gy', 'gz'), may hold values from 0 to 1
- volume: float32 [4, 2, 4, 864, 128], P('gx', 'gy', 'gz'), may hold values from 0.005 to 0.05
Outputs:
- forces: float32 [3, 16, 8, 8, 128], P(None, 'gx', 'gy', 'gz')
- film_next: float32 [16, 8, 8, 128], P('gx', 'gy', 'gz')
- volume_next: float32 [4, 2, 4, 864, 128], P('gx', 'gy', 'gz')
Inputs may be any that keep to these rules, and one draw needn't show every extreme that they name: `pair_live`: slot s of a device is 1 only if its tile pair lies inside the grid; every pair of distinct touching tiles is listed at most once over all devices, by one of its two tiles; the slot of a tile with itself (s % 27 = 13) is always 1. partner[s, m] is never m itself. `positions`: the grains of tile (p, q, r) lie in its box, 8 wide along the first dimension and 4 along the others, the boxes side by side from the root; no two grains are closer than 0.5.
All inputs are finite; a program needn't handle non-finite values.
Results may differ from a plain program's by a relative error of at most 0.0003.
Values sent between devices are 32-bit elements; how exact they have to be, the bound alone decides.
A program may use at most 64 MiB of HBM per device.

v0:
```python
import functools

import jax
import jax.numpy as jnp
from jax import lax
from jax.experimental import pallas as pl
from jax.experimental.pallas import tpu as pltpu
from jax.sharding import PartitionSpec as P

ABSORB = 0.02
TINY = 1e-30
RADIUS_MAX = 0.6
SLACK = 4e-3
AWAY = -1e4
FLOOR = 1e-12


def neighbours():
    found = [
        (ex, ey, ez)
        for ex in (-1, 0, 1)
        for ey in (-1, 0, 1)
        for ez in (-1, 0, 1)
        if (ex, ey, ez) != (0, 0, 0)
    ]
    return sorted(found, key=lambda offset: -sum(map(abs, offset)))


AXES = ("gx", "gy", "gz")


def present(offset):
    found = None
    for axis, shift in zip(AXES, offset):
        if shift == 0:
            continue
        place = lax.axis_index(axis) + shift
        here = (place >= 0) & (place < lax.axis_size(axis))
        found = here if found is None else found & here
    return found


def device_at(offset):
    return tuple(lax.axis_index(axis) + shift for axis, shift in zip(AXES, offset))


def opposite(offset):
    return tuple(-shift for shift in offset)


def greet(offsets):
    barrier = pltpu.get_barrier_semaphore()
    count = jnp.int32(0)
    for offset in offsets:
        here = present(offset)
        count = count + here.astype(jnp.int32)

        @pl.when(here)
        def _():
            pl.semaphore_signal(
                barrier, inc=1, device_id=device_at(offset), device_id_type=pl.DeviceIdType.MESH
            )

    pl.semaphore_wait(barrier, count)


def cut(offset, extents, low, whole, high):
    pick = []
    for shift, extent in zip(offset, extents):
        if shift < 0:
            pick.append(pl.ds(low(extent), 1))
        elif shift > 0:
            pick.append(pl.ds(high(extent), 1))
        else:
            pick.append(pl.ds(whole, extent))
    return (slice(None),) + tuple(pick)


def rim(offset, extents):
    return cut(offset, extents, lambda n: 0, 1, lambda n: n + 1)


def edge(offset, extents):
    return cut(offset, extents, lambda n: 0, 0, lambda n: n - 1)


def spread_kernel(
    extents, place_ref, radius_ref, film_ref, border_ref, state, blank, local_sem, send_sem, recv_sem
):
    offsets = neighbours()
    loads = [
        pltpu.make_async_copy(place_ref, state.at[pl.ds(0, 3)], local_sem.at[0]),
        pltpu.make_async_copy(radius_ref, state.at[pl.ds(3, 1)], local_sem.at[1]),
        pltpu.make_async_copy(film_ref, state.at[pl.ds(4, 1)], local_sem.at[2]),
    ]
    for load in loads:
        load.start()
    greet(offsets)
    blank[...] = jnp.zeros_like(blank)
    for load in loads:
        load.wait()
    copies, fills = [], []
    for i, offset in enumerate(offsets):
        copy = pltpu.make_async_remote_copy(
            src_ref=state.at[edge(offset, extents)],
            dst_ref=border_ref.at[rim(opposite(offset), extents)],
            send_sem=send_sem.at[i],
            recv_sem=recv_sem.at[i],
            device_id=device_at(offset),
            device_id_type=pl.DeviceIdType.MESH,
        )
        copies.append(copy)
        pl.when(present(offset))(copy.start)
    inner = pltpu.make_async_copy(
        state, border_ref.at[rim((0, 0, 0), extents)], local_sem.at[3]
    )
    inner.start()
    for i, offset in enumerate(offsets):
        fill = pltpu.make_async_copy(
            blank.at[edge(offset, extents)],
            border_ref.at[rim(offset, extents)],
            local_sem.at[4 + i],
        )
        fills.append(fill)
        pl.when(jnp.logical_not(present(offset)))(fill.start)
    inner.wait()
    for offset, copy, fill in reversed(list(zip(offsets, copies, fills))):
        pl.when(jnp.logical_not(present(offset)))(fill.wait)
        pl.when(present(offset))(copy.wait_send)
        pl.when(present(opposite(offset)))(copy.wait_recv)


def return_kernel(extents, totals_ref, sum_ref, *scratch):
    offsets = neighbours()
    inbox, (inner, local_sem, send_sem, recv_sem) = scratch[:-4], scratch[-4:]
    load = pltpu.make_async_copy(totals_ref.at[rim((0, 0, 0), extents)], inner, local_sem)
    load.start()
    greet(offsets)
    copies = []
    for i, offset in enumerate(offsets):
        copy = pltpu.make_async_remote_copy(
            src_ref=totals_ref.at[rim(offset, extents)],
            dst_ref=inbox[i],
            send_sem=send_sem.at[i],
            recv_sem=recv_sem.at[i],
            device_id=device_at(offset),
            device_id_type=pl.DeviceIdType.MESH,
        )
        copies.append(copy)
        pl.when(present(offset))(copy.start)
    load.wait()
    sum_ref[...] = inner[...]
    order = sorted(range(len(offsets)), key=lambda i: sum(map(abs, offsets[i])))
    for i in order:
        offset, copy = offsets[i], copies[i]

        @pl.when(present(opposite(offset)))
        def _():
            copy.wait_recv()
            region = edge(opposite(offset), extents)
            sum_ref[region] = sum_ref[region] + inbox[i][...]

    for offset, copy in zip(offsets, copies):
        pl.when(present(offset))(copy.wait_send)


def finish_kernel(sum_ref, film_ref, force_ref, next_ref):
    count = force_ref.shape[0]
    force_ref[...] = sum_ref[0:count, :]
    next_ref[...] = film_ref[...] + sum_ref[count:, :]


def spread(place, radius, film, extents):
    sems = pltpu.SemaphoreType.DMA((26,))
    anywhere = pl.BlockSpec(memory_space=pl.ANY)
    tail = place.shape[4:]
    shape = (5,) + tuple(n + 2 for n in extents) + tail
    own = pltpu.VMEM((5,) + tuple(extents) + tail, jnp.float32)
    return pl.pallas_call(
        functools.partial(spread_kernel, extents),
        out_shape=jax.ShapeDtypeStruct(shape, jnp.float32),
        in_specs=[anywhere] * 3,
        out_specs=anywhere,
        scratch_shapes=[own, own, pltpu.SemaphoreType.DMA((30,)), sems, sems],
        compiler_params=pltpu.CompilerParams(collective_id=0, has_side_effects=True),
        name="spread",
    )(place, radius, film)


def collect(totals, extents):
    sems = pltpu.SemaphoreType.DMA((26,))
    vmem = pl.BlockSpec(memory_space=pltpu.VMEM)
    tail = totals.shape[4:]
    boxes = [
        pltpu.VMEM(
            (4,) + tuple(1 if e else n for e, n in zip(offset, extents)) + tail, jnp.float32
        )
        for offset in neighbours()
    ]
    return pl.pallas_call(
        functools.partial(return_kernel, extents),
        out_shape=jax.ShapeDtypeStruct((4,) + tuple(extents) + tail, jnp.float32),
        in_specs=[pl.BlockSpec(memory_space=pl.ANY)],
        out_specs=vmem,
        scratch_shapes=boxes
        + [
            pltpu.VMEM((4,) + tuple(extents) + tail, jnp.float32),
            pltpu.SemaphoreType.DMA,
            sems,
            sems,
        ],
        compiler_params=pltpu.CompilerParams(collective_id=1, has_side_effects=True),
        name="collect",
    )(totals)


def split(values):
    high = values.astype(jnp.bfloat16)
    low = (values - high.astype(jnp.float32)).astype(jnp.bfloat16)
    return high, low


def take(values, index):
    return jnp.take_along_axis(
        values, index, axis=1, mode="promise_in_bounds", wrap_negative_indices=False
    )


def kernel(
    dims,
    border_hbm,
    live_ref,
    partner_ref,
    rupture_ref,
    volume_ref,
    totals_ref,
    fresh_ref,
    others,
    flags,
    wide,
    triangle,
    held,
    mask,
    before,
    probes,
    offset,
    place,
    lists,
    summed,
    owned,
    table_even,
    table_odd,
    table_more,
    acc,
    near,
    far,
    counts,
    todo,
    agenda,
    agenda_sem,
    border_ref,
    border_sem,
):
    bx, by, bz, grains = dims
    tables = (table_even, table_odd)
    wy, wz = by + 2, bz + 2
    plane = by * bz
    step = pl.program_id(0)
    cells = (bx + 2) * wy * wz
    f32 = jnp.float32
    faces = [4, 22, 10, 16, 12, 14]
    outer = [s for s in range(27) if s != 13 and s not in faces] + faces

    def other_row(x, j, c):
        return pl.multiple_of(((x * 9 + j) * 6 + c) * plane, plane)

    deep = -(-wy * bz // 8) * 8

    def far_base(x, ez, c):
        return pl.multiple_of(((ez * (bx + 2) + x) * 4 + c) * deep, 8)

    def far_line(x, j, c):
        return pl.ds(far_base(x, j % 3, c) + j // 3 * bz, plane)

    def enlist():
        shape = (bx * plane, grains)
        dims_p = (((1,), (0,)), ((), ()))
        listed = flags[...].astype(jnp.bfloat16)
        ahead = lax.dot_general(
            listed, triangle[:, 0 : 2 * grains], dims_p, preferred_element_type=f32
        )
        amount = ahead[:, grains : 2 * grains].astype(jnp.int32)
        ahead = ahead[:, 0:grains].astype(jnp.int32)
        at = lax.broadcasted_iota(jnp.int32, shape, 1)
        rank = at & 31
        slot = jnp.zeros(shape, jnp.int32)
        for bit in (16, 8, 4, 2, 1):
            slot = jnp.where(take(ahead, slot + (bit - 1)) <= rank, slot + bit, slot)
        valid = rank < amount

        def parts(value, size, number):
            high = sum((value >= size * n).astype(jnp.int32) for n in range(1, number))
            return high, value - size * high

        ix, local = parts(lax.broadcasted_iota(jnp.int32, shape, 0), plane, bx)
        iy, iz = parts(local, bz, by)
        ex, rest = parts(slot, 9, 3)
        ey, ez = parts(rest, 3, 3)
        cell = ((ix + ex) * wy + iy + ey) * wz + iz + ez
        line = local * 27 + slot
        first = jnp.where(valid, line, 0)
        second = jnp.where(valid, line * 8, 27 * plane * 8)
        third = jnp.where(valid, cell * 8, cells * 8)
        low = jnp.where(at < 32, first, second)
        high = jnp.where(at < 96, third, amount)
        todo[...] = jnp.where(at < 64, low, high)
        pltpu.make_async_copy(todo, agenda, agenda_sem).start()

    @pl.when(step == 0)
    def _():
        fetch = pltpu.make_async_copy(border_hbm, border_ref, border_sem)
        fetch.start()
        near[...] = jnp.zeros_like(near)
        far[...] = jnp.zeros_like(far)
        summed[...] = jnp.zeros_like(summed)
        held[27 * plane * 8 :, :] = jnp.zeros((8, grains), f32)
        rows = lax.broadcasted_iota(jnp.int32, (grains, grains), 0)
        cols = lax.broadcasted_iota(jnp.int32, (grains, grains), 1)
        half = grains // 2
        for n, last in enumerate((cols, grains, half - 1, half // 2 - 1, half + half // 2 - 1)):
            block = (rows <= last).astype(f32).astype(jnp.bfloat16)
            triangle[:, n * grains : (n + 1) * grains] = block
        flags[...] = jnp.zeros_like(flags)
        for t in range(bx * plane):
            flags[t : t + 1, 0:27] = live_ref[0:1, t * 27 : t * 27 + 27].astype(f32)

        def widen(x, carry):
            row = flags[pl.ds(pl.multiple_of(x * plane, plane), plane), :]
            for s in range(27):
                line = pl.ds(pl.multiple_of((x * 27 + s) * plane, plane), plane)
                wide[line, :] = jnp.broadcast_to(row[:, s : s + 1], (plane, grains))
            return carry

        lax.fori_loop(0, bx, widen, 0)

        def arrange(x, carry):
            for j in range(9):
                ey, ez = j // 3, j % 3
                for c in range(5):
                    for z in range(bz):
                        start = c * cells + (x * wy + ey) * wz + z + ez
                        got = border_ref[pl.ds(start, by, stride=wz), :]
                        others[pl.ds(((x * 9 + j) * 6 + c) * plane + z, by, stride=bz), :] = got
            for j in range(9):
                radius = others[pl.ds(other_row(x, j, 3), plane), :]
                others[pl.ds(other_row(x, j, 5), plane), :] = 1.0 / radius
            return carry

        enlist()
        fetch.wait()
        lax.fori_loop(0, bx + 2, arrange, 0)

    def cell_at(tile):
        x, local = tile // plane, tile % plane
        return ((x + 1) * wy + local // bz + 1) * wz + local % bz + 1

    def plane_of(x):
        return pl.ds(pl.multiple_of(x * plane, plane), plane)

    def lit(x, s):
        return wide[pl.ds(pl.multiple_of((x * 27 + s) * plane, plane), plane), :]

    def prescan(x):
        mine = [others[pl.ds(other_row(x + 1, 4, c), plane), :] for c in range(4)]
        highs = [jnp.max(mine[c], axis=1, keepdims=True) for c in range(3)]
        lows = [jnp.min(mine[c], axis=1, keepdims=True) for c in range(3)]
        widest = jnp.max(mine[3], axis=1, keepdims=True) + SLACK
        def select(s):
            part = slice(s * plane, (s + 1) * plane)
            if s == 13:
                mask[part, :] = jnp.zeros((plane, grains), f32)
                return
            there = [others[pl.ds(other_row(x + s // 9, s % 9, c), plane), :] for c in range(4)]
            away = [
                jnp.maximum(jnp.maximum(lows[c] - there[c], there[c] - highs[c]), 0.0)
                for c in range(3)
            ]
            reach = widest + there[3]
            inside = away[0] * away[0] + away[1] * away[1] + away[2] * away[2] < reach * reach
            mask[part, :] = jnp.where(inside, lit(x, s), 0.0)

        return select

    def scan(slot):
        prefix = lax.dot_general(
            mask[...].astype(jnp.bfloat16),
            triangle[...],
            (((1,), (0,)), ((), ())),
            preferred_element_type=f32,
        )
        total = jnp.zeros((plane, grains), f32)
        for i, s in enumerate(outer):
            part = slice(s * plane, (s + 1) * plane)
            ahead = prefix[part, 0:grains]
            before[slot, part, :] = ahead
            for n in range(3):
                probes[slot, n, part, :] = prefix[part, (n + 2) * grains : (n + 3) * grains]
            offset[slot, i * plane : (i + 1) * plane, :] = total
            spot = jnp.where(mask[part, :] > 0.0, total + ahead - 1.0, -1.0)
            place[slot, part, :] = spot.astype(jnp.int32)
            if i == len(outer) - 4:
                counts[slot, plane + 1] = jnp.max(total).astype(jnp.int32)
            total = total + prefix[part, grains : 2 * grains]
        offset[slot, 26 * plane : 27 * plane, :] = total
        for t in range(plane):
            counts[slot, t] = total[t, 0].astype(jnp.int32)
        counts[slot, plane] = jnp.max(total).astype(jnp.int32)

    now = step % 2
    lane = lax.broadcasted_iota(jnp.int32, (plane, grains), 1)

    def build(group, beside, first, into, after=()):
        wanted = (lane + group * grains).astype(f32)
        half = grains // 2
        index = {}
        bit = half // 2
        level = 0
        while bit:
            for i, s in list(enumerate(outer))[first:]:
                part = slice(s * plane, (s + 1) * plane)
                rank = wanted - offset[now, i * plane : (i + 1) * plane, :]
                if bit == half // 2:
                    upper = probes[now, 0, part, :] <= rank
                    probe = jnp.where(upper, probes[now, 2, part, :], probes[now, 1, part, :])
                    index[s] = jnp.where(upper, half, 0)
                else:
                    probe = take(before[now, part, :], index[s] + (bit - 1))
                index[s] = jnp.where(probe <= rank, index[s] + bit, index[s])
            for work in beside[level::6]:
                work()
            bit //= 2
            level += 1
        for work in after:
            work()
        found = [jnp.full((plane, grains), AWAY, f32)] * 3 + [jnp.full((plane, grains), 0.5, f32)]
        for i, s in list(enumerate(outer))[first:]:
            low = offset[now, i * plane : (i + 1) * plane, :]
            high = offset[now, (i + 1) * plane : (i + 2) * plane, :]
            here = (wanted >= low) & (wanted < high)
            for c in range(4):
                member = others[pl.ds(other_row(step + s // 9, s % 9, c), plane), :]
                found[c] = jnp.where(here, take(member, index[s]), found[c])
        for c, member in enumerate(found + [1.0 / found[3]]):
            lists[into, c * plane : (c + 1) * plane, :] = member

    @pl.when(step == 0)
    def _():
        select = prescan(0)
        for s in range(27):
            select(s)
        scan(0)

    own = [others[pl.ds(other_row(step + 1, 4, c), plane), :] for c in range(5)]
    twice = 2.0 * own[3]
    sums = [jnp.zeros((plane, grains), f32)] * 4
    select = prescan(jnp.minimum(step + 1, bx - 1))

    def bridge(s):
        near_by = [others[pl.ds(other_row(step + s // 9, s % 9, c), plane), :] for c in range(5)]
        lines = pl.ds(s, plane, stride=27)
        partner = partner_ref[lines, :]
        got = [take(member, partner) for member in near_by]
        active = lit(step, s)
        gap = [own[c] - got[c] for c in range(3)]
        square = gap[0] * gap[0] + gap[1] * gap[1] + gap[2] * gap[2]
        inverse = lax.rsqrt(square)
        radius_sum = own[3] + got[3]
        product = twice * got[3]
        vol = volume_ref[lines, :]
        root = product * lax.rsqrt(product * (radius_sum * vol))
        scaled = jnp.maximum(square * inverse - radius_sum, 0.0) * root
        broken = rupture_ref[lines, :].astype(f32)
        intact = active * (1.0 - broken)
        curve = 1.0 + scaled * (1.05 + 2.5 * scaled)
        tension = jnp.where(intact > 0.0, product * inverse / (radius_sum * curve), 0.0)
        force = [tension * member for member in gap]
        released = 0.5 * active * broken * vol
        soaked = ABSORB * intact
        from_own = soaked * own[4]
        from_got = soaked * got[4]
        fresh_ref[lines, :] = intact * vol + (from_own + from_got)
        for c, member in enumerate(force + [released - from_got]):
            high = member.astype(jnp.bfloat16).astype(f32)
            held[pl.ds(s * 8 + c, plane, stride=27 * 8), :] = high
            held[pl.ds(s * 8 + c + 4, plane, stride=27 * 8), :] = member - high
        for c in range(3):
            sums[c] = sums[c] - force[c]
        sums[3] = sums[3] + (released - from_own)
        select(s)

    build(
        0,
        [functools.partial(bridge, s) for s in range(27)],
        0,
        0,
        [functools.partial(scan, 1 - now)],
    )
    for c in range(4):
        owned[c] = sums[c]
    most = counts[now, plane]

    def distribute(group, first, into):
        rows = [summed[into, c * plane : (c + 1) * plane, :] for c in range(3)]
        for s in outer[first:]:
            spot = place[now, s * plane : (s + 1) * plane, :] - group * grains
            here = (spot >= 0) & (spot < grains)
            index = spot & (grains - 1)
            for c in range(3):
                moved = jnp.where(here, take(rows[c], index), 0.0)
                line = far_line(step + s // 9, s % 9, c)
                far[line, :] = far[line, :] - moved

    def own_row(tile, c):
        x, local = tile // plane, tile % plane
        return (((x + 1) * 9 + 4) * 6 + c) * plane + local

    def columns_of(tile):
        block = others[pl.ds(own_row(tile, 0), 6, stride=plane), :]
        return jnp.concatenate([block, jnp.zeros((2, grains), f32)], axis=0).T

    def spread_columns(table, columns, m):
        for at in range(5 * m, 5 * m + 5):
            n, block = at // (grains // 8), at % (grains // 8)
            c = (0, 1, 2, 3, 5)[n]
            part = slice(8 * block, 8 * block + 8)
            table[n, part] = jnp.broadcast_to(columns[part, c : c + 1], (8, grains))

    def pushes(mine, theirs, own_tile):
        deltas = [mine[c] - theirs[c] for c in range(3)]
        square = deltas[0] * deltas[0] + deltas[1] * deltas[1] + deltas[2] * deltas[2]
        if own_tile:
            square = jnp.maximum(square, FLOOR)
        inverse = lax.rsqrt(square)
        inter = jnp.maximum(mine[3] + theirs[3] - square * inverse, TINY)
        push = inter * inter * inverse * lax.rsqrt(inter * (mine[4] + theirs[4]))
        return [push * member for member in deltas]

    def contacts(local, table, groups, own_tile, beside):
        listed = [
            [
                jnp.broadcast_to(lists[g, pl.ds(c * plane + local, 1), :], (8, grains))
                for c in range(5)
            ]
            for g in groups
        ]
        selves = [
            jnp.broadcast_to(others[pl.ds(own_row(step * plane + local, c), 1), :], (8, grains))
            for c in (0, 1, 2, 3, 5)
        ]
        collected = [[jnp.zeros((8, grains), f32)] * 3 for g in groups]
        for m in range(grains // 8):
            part = slice(8 * m, 8 * m + 8)
            mine = [table[c, part] for c in range(5)]
            both = pushes(mine, selves, True) if own_tile else None
            for g, theirs in enumerate(listed):
                products = pushes(mine, theirs, False)
                for c in range(3):
                    collected[g][c] = collected[g][c] + products[c]
                both = [a + b for a, b in zip(both, products)] if both else products
            for c in range(3):
                acc[c, part] = both[c]
            beside(m)
        for g, into in enumerate(groups):
            for c in range(3):
                line = jnp.sum(collected[g][c], axis=0, keepdims=True)
                summed[into, pl.ds(c * plane + local, 1), :] = line
        ones = jnp.ones((8, 2 * grains), jnp.bfloat16)
        for c in range(3):
            both = jnp.concatenate(split(acc[c]), axis=1)
            value = lax.dot_general(ones, both, across, preferred_element_type=f32)
            line = pl.ds(local, 1)
            owned[c, line, :] = owned[c, line, :] + value[0:1]

    across = (((1,), (1,)), ((), ()))
    lanes = lax.broadcasted_iota(jnp.int32, (grains, grains), 0).astype(f32).astype(jnp.bfloat16)
    one = jnp.ones((grains, grains), jnp.bfloat16)
    zero = jnp.zeros((grains, grains), jnp.bfloat16)
    blank = jnp.zeros((8, grains), jnp.bfloat16)

    def bridges(local, pair):
        chosen, left, targets = [], [], []
        tile = step * plane + local
        for k in (2 * pair, 2 * pair + 1):
            targets.append(agenda[tile, 64 + k])
            left.append(held[pl.ds(pl.multiple_of(agenda[tile, 32 + k], 8), 8), :])
            aim = partner_ref[pl.ds(agenda[tile, k], 1), :]
            aim = jnp.broadcast_to(aim.astype(f32).astype(jnp.bfloat16), (grains, grains))
            chosen.append(jnp.where(lanes == aim, one, zero))
        none = jnp.zeros((8, grains), f32)
        first = jnp.concatenate([left[0], none], axis=0).astype(jnp.bfloat16)
        second = jnp.concatenate([none, left[1]], axis=0).astype(jnp.bfloat16)
        moved = lax.dot_general(
            jnp.concatenate([first, second], axis=1),
            jnp.concatenate(chosen, axis=1),
            across,
            preferred_element_type=f32,
        )
        for n, target in enumerate(targets):
            rows = pl.ds(pl.multiple_of(target, 8), 8)
            near[rows, :] = near[rows, :] + moved[8 * n : 8 * n + 8]

    @pl.when(step == 0)
    def _():
        columns = columns_of(0)
        for m in range(grains // 8):
            spread_columns(tables[0], columns, m)

    early = counts[now, plane + 1]

    @pl.when((most > grains) & (early > grains))
    def _():
        build(1, [], 0, 1)

    @pl.when((most > grains) & (early <= grains))
    def _():
        build(1, [], 22, 1)

    def tile_step(couple, carry):
        def run(groups):
            for half in range(2):
                local = 2 * couple + half
                tile = step * plane + local
                columns = columns_of(jnp.minimum(tile + 1, bx * plane - 1))

                def beside(m):
                    spread_columns(tables[1 - half], columns, m)
                    if m % 2 == 0:
                        bridges(local, m // 2)

                contacts(local, tables[half], groups, True, beside)

        crowded = jnp.maximum(counts[now, 2 * couple], counts[now, 2 * couple + 1]) > grains

        @pl.when(crowded)
        def _():
            run((0, 1))

        @pl.when(jnp.logical_not(crowded))
        def _():
            run((0,))

        for half in range(2):
            local = 2 * couple + half

            def spare(pair, inner):
                bridges(local, pair)
                return inner

            lax.fori_loop(grains // 16, (agenda[step * plane + local, 96] + 1) // 2, spare, 0)
        return carry

    @pl.when(step == 0)
    def _():
        pltpu.make_async_copy(todo, agenda, agenda_sem).wait()

    lax.fori_loop(0, plane // 2, tile_step, 0)
    distribute(0, 0, 0)

    @pl.when((most > grains) & (early > grains))
    def _():
        distribute(1, 0, 1)

    @pl.when((most > grains) & (early <= grains))
    def _():
        distribute(1, 22, 1)

    def more(group, carry):
        build(group, [], 0, 0)

        def again(local, inner):
            @pl.when(counts[now, local] > group * grains)
            def _():
                columns = columns_of(step * plane + local)
                for m in range(grains // 8):
                    spread_columns(table_more, columns, m)
                contacts(local, table_more, (0,), False, lambda m: None)

            return inner

        lax.fori_loop(0, plane, again, 0)
        distribute(group, 0, 0)
        return carry

    lax.fori_loop(2, (most + grains - 1) // grains, more, 0)
    for c in range(4):
        line = far_line(step + 1, 4, c)
        far[line, :] = far[line, :] + owned[c]

    @pl.when(step == pl.num_programs(0) - 1)
    def _():
        def fold(x, carry):
            sheet = wy * wz
            for c in range(4):
                base = pl.multiple_of(x * (sheet * 8), 8)
                value = near[pl.ds(base + c, sheet, stride=8), :]
                value = value + near[pl.ds(base + c + 4, sheet, stride=8), :]
                totals_ref[pl.ds(c * cells + x * sheet, sheet), :] = value
                for ez in range(3) if c < 3 else (1,):
                    for z in range(bz):
                        line = pl.ds(c * cells + x * sheet + z + ez, wy, stride=wz)
                        add = far[pl.ds(far_base(x, ez, c) + z, wy, stride=bz), :]
                        totals_ref[line, :] = totals_ref[line, :] + add
            return carry

        lax.fori_loop(0, bx + 2, fold, 0)


def shards(positions, grain_radii, film_liquid, pair_live, partner, rupture, volume):
    bx, by, bz, grains = grain_radii.shape
    tiles = bx * by * bz
    slots = 27 * tiles
    cells = (bx + 2) * (by + 2) * (bz + 2)
    extents = (bx, by, bz)
    film = film_liquid.reshape(1, bx, by, bz, 1, grains)
    border = spread(
        positions.reshape(3, bx, by, bz, 1, grains),
        grain_radii.reshape(1, bx, by, bz, 1, grains),
        film,
        extents,
    ).reshape(5 * cells, grains)
    plane = by * bz
    span = 27 * plane
    wide = pl.BlockSpec((span, grains), lambda i: (i, 0))
    f32 = jnp.float32
    totals, fresh = pl.pallas_call(
        functools.partial(kernel, (bx, by, bz, grains)),
        grid_spec=pltpu.PrefetchScalarGridSpec(
            num_scalar_prefetch=0,
            grid=(bx,),
            in_specs=[
                pl.BlockSpec(memory_space=pl.ANY),
                pl.BlockSpec((1, slots), lambda i: (0, 0)),
                wide,
                wide,
                wide,
            ],
            out_specs=[pl.BlockSpec((4 * cells, grains), lambda i: (0, 0)), wide],
            scratch_shapes=[
                pltpu.VMEM(((bx + 2) * 9 * 6 * plane, grains), f32),
                pltpu.VMEM((tiles, grains), f32),
                pltpu.VMEM((slots, grains), f32),
                pltpu.VMEM((grains, 5 * grains), jnp.bfloat16),
                pltpu.VMEM((span * 8 + 8, grains), f32),
                pltpu.VMEM((span, grains), f32),
                pltpu.VMEM((2, span, grains), f32),
                pltpu.VMEM((2, 3, span, grains), f32),
                pltpu.VMEM((2, span + plane, grains), f32),
                pltpu.VMEM((2, span, grains), jnp.int32),
                pltpu.VMEM((2, 5 * plane, grains), f32),
                pltpu.VMEM((2, 3 * plane, grains), f32),
                pltpu.VMEM((4, plane, grains), f32),
                pltpu.VMEM((5, grains, grains), f32),
                pltpu.VMEM((5, grains, grains), f32),
                pltpu.VMEM((5, grains, grains), f32),
                pltpu.VMEM((3, grains, grains), f32),
                pltpu.VMEM((cells * 8 + 8, grains), f32),
                pltpu.VMEM((3 * (bx + 2) * 4 * (-(-(by + 2) * bz // 8) * 8), grains), f32),
                pltpu.SMEM((2, plane + 2), jnp.int32),
                pltpu.VMEM((tiles, grains), jnp.int32),
                pltpu.SMEM((tiles, grains), jnp.int32),
                pltpu.SemaphoreType.DMA,
                pltpu.VMEM((5 * cells, grains), f32),
                pltpu.SemaphoreType.DMA,
            ],
        ),
        out_shape=[
            jax.ShapeDtypeStruct((4 * cells, grains), f32),
            jax.ShapeDtypeStruct((slots, grains), f32),
        ],
        name="slots",
    )(
        border,
        pair_live.reshape(1, slots),
        partner.reshape(slots, grains),
        rupture.reshape(slots, grains),
        volume.reshape(slots, grains),
    )
    totals = totals.reshape(4, bx + 2, by + 2, bz + 2, 1, grains)
    summed = collect(totals, extents).reshape(4 * tiles, grains)
    vmem = pl.BlockSpec(memory_space=pltpu.VMEM)
    forces, film_next = pl.pallas_call(
        finish_kernel,
        out_shape=[
            jax.ShapeDtypeStruct((3 * tiles, grains), f32),
            jax.ShapeDtypeStruct((tiles, grains), f32),
        ],
        in_specs=[vmem, vmem],
        out_specs=[vmem, vmem],
        name="finish",
    )(summed, film_liquid.reshape(tiles, grains))
    return (
        forces.reshape(positions.shape),
        film_next.reshape(film_liquid.shape),
        fresh.reshape(volume.shape),
    )


def solution(mesh):
    return jax.shard_map(
        shards,
        mesh=mesh,
        in_specs=(
            P(None, "gx", "gy", "gz", None),
            P("gx", "gy", "gz", None),
            P("gx", "gy", "gz", None),
            P("gx", "gy", "gz", None),
            P("gx", "gy", "gz", None, None),
            P("gx", "gy", "gz", None, None),
            P("gx", "gy", "gz", None, None),
        ),
        out_specs=(
            P(None, "gx", "gy", "gz", None),
            P("gx", "gy", "gz", None),
            P("gx", "gy", "gz", None, None),
        ),
        check_vma=False,
    )
```

profile of v0, /device:TPU:0, one launch (start us, length us, event | category | flops | bytes accessed | tf_op | source)
XLA Modules:
  0.0 41.8 jit_solution(13783536891684159709)
XLA Ops:
  0.6 9.4 %spread.1 = f32[5,6,6,4,1,128]{5,4,3,2,1,0:T(1,128)} custom-call(f32[3,4,4,2,1,128]{5,4,3,2,1,0:T(1,128)} %bitcast.22, f32[1,4,4,2,1,128]{5,4,3,2,1,0:T(1,128)} %bitcast.23, f32[1,4,4,2,1,128]{5,4,3,2,1,0:T(1,128)} %bitcast.20), custom_call_target="tpu_custom_call" | custom-call | tf_op jit(solution)/shard_map/spread/pallas_call | solution.py:179
  10.1 22.3 %slots.1 = (f32[576,128]{1,0:T(8,128)}, f32[864,128]{1,0:T(8,128)}) custom-call(f32[720,128]{1,0:T(8,128)} %bitcast.14, s32[1,864]{1,0:T(1,128)} %bitcast.24, s32[864,128]{1,0:T(8,128)} %bitcast.15, s32[864,128]{1,0:T(8,128)} %bitcast.16, f32[864,128]{1,0:T(8,128)} %bitcast.17), custom_call_target="tpu_custom_call" | custom-call | tf_op jit(solution)/shard_map/slots/pallas_call | solution.py:735
  32.4 8.0 %collect.1 = f32[4,4,4,2,1,128]{5,4,3,2,1,0:T(1,128)} custom-call(f32[4,6,6,4,1,128]{5,4,3,2,1,0:T(1,128)} %bitcast.18), custom_call_target="tpu_custom_call" | custom-call | tf_op jit(solution)/shard_map/collect/pallas_call | solution.py:200
  40.4 1.5 %finish.1 = (f32[96,128]{1,0:T(8,128)}, f32[32,128]{1,0:T(8,128)}) custom-call(f32[128,128]{1,0:T(8,128)} %bitcast.19, f32[32,128]{1,0:T(8,128)} %bitcast.21), custom_call_target="tpu_custom_call" | custom-call | tf_op jit(solution)/shard_map/finish/pallas_call | solution.py:791
where the time goes:
time: 41.3 us; the launch traced here: 41.8 us
  Pallas kernels  41.2 us (100%)
  between operations  0.65 us (2%)
    pallas_call x1, Pallas kernels, shards(): pl.pallas_call(functools.partial(kernel, (bx, by, bz, grains)), grid_spec...  22.3 us
    pallas_call x1, Pallas kernels, spread(): pl.pallas_call(functools.partial(spread_kernel, extents), out_shape=jax.S...  9.42 us
    pallas_call x1, Pallas kernels, collect(): pl.pallas_call(functools.partial(return_kernel, extents), out_shape=jax.S...  7.98 us
    pallas_call x1, Pallas kernels, shards(): pl.pallas_call(finish_kernel, out_shape=[jax.ShapeDtypeStruct((3 * tiles,...  1.47 us

commit v1 on v0

--- a/solution.py
+++ b/solution.py
@@ -1,4 +1,5 @@
 import functools
+import math
 
 import jax
 import jax.numpy as jnp
@@ -48,7 +49,7 @@
     return tuple(-shift for shift in offset)
 
 
-def greet(offsets):
+def greet(offsets, meanwhile=None):
     barrier = pltpu.get_barrier_semaphore()
     count = jnp.int32(0)
     for offset in offsets:
@@ -61,6 +62,8 @@
                 barrier, inc=1, device_id=device_at(offset), device_id_type=pl.DeviceIdType.MESH
             )
 
+    if meanwhile:
+        meanwhile()
     pl.semaphore_wait(barrier, count)
 
 
@@ -84,18 +87,96 @@
     return cut(offset, extents, lambda n: 0, 0, lambda n: n - 1)
 
 
+def pushes(mine, theirs, own_tile):
+    deltas = [mine[c] - theirs[c] for c in range(3)]
+    square = deltas[0] * deltas[0] + deltas[1] * deltas[1] + deltas[2] * deltas[2]
+    if own_tile:
+        square = jnp.maximum(square, FLOOR)
+    inverse = lax.rsqrt(square)
+    inter = jnp.maximum(mine[3] + theirs[3] - square * inverse, TINY)
+    push = inter * inter * inverse * lax.rsqrt(inter * (mine[4] + theirs[4]))
+    return [push * member for member in deltas]
+
+
 def spread_kernel(
-    extents, place_ref, radius_ref, film_ref, border_ref, state, blank, local_sem, send_sem, recv_sem
+    extents,
+    place_ref,
+    radius_ref,
+    film_ref,
+    flat_place_ref,
+    flat_radius_ref,
+    border_ref,
+    inner_ref,
+    state,
+    blank,
+    flat,
+    picker,
+    local_sem,
+    flat_sem,
+    send_sem,
+    recv_sem,
 ):
     offsets = neighbours()
+    tiles, grains = flat_radius_ref.shape
+    flats = [
+        pltpu.make_async_copy(flat_place_ref, flat.at[pl.ds(0, 3 * tiles)], flat_sem.at[0]),
+        pltpu.make_async_copy(flat_radius_ref, flat.at[pl.ds(3 * tiles, tiles)], flat_sem.at[1]),
+    ]
+
+    def rows_of(tile):
+        block = flat[pl.ds(tile, 4, stride=tiles), :]
+        rows = [block[c : c + 1] for c in range(4)]
+        return rows + [1.0 / rows[3]]
+
+    def own_contacts(batch, carry):
+        for n in range(4):
+            tile = 4 * batch + n
+            rows = rows_of(tile)
+            block = jnp.concatenate(rows + [jnp.zeros((3, grains), jnp.float32)], axis=0)
+            pieces = []
+            for _ in range(3):
+                piece = block.astype(jnp.bfloat16).astype(jnp.float32)
+                pieces.append(piece)
+                block = block - piece
+            columns = jnp.concatenate(pieces + [jnp.zeros((8, grains), jnp.float32)], axis=0).T
+            table = lax.dot_general(
+                columns.astype(jnp.bfloat16),
+                picker[...],
+                (((1,), (0,)), ((), ())),
+                preferred_element_type=jnp.float32,
+            )
+            theirs = [jnp.broadcast_to(row, (8, grains)) for row in rows]
+            total = [jnp.zeros((8, grains), jnp.float32)] * 3
+            for m in range(grains // 8):
+                part = slice(8 * m, 8 * m + 8)
+                mine = [table[part, c * grains : (c + 1) * grains] for c in range(5)]
+                for c, member in enumerate(pushes(mine, theirs, True)):
+                    total[c] = total[c] - member
+            for c in range(3):
+                line = jnp.sum(total[c], axis=0, keepdims=True)
+                inner_ref[pl.ds(c * tiles + tile, 1), :] = line
+        return carry
+
+    batches = tiles // 4
+    early = 3 * batches // 8
     loads = [
         pltpu.make_async_copy(place_ref, state.at[pl.ds(0, 3)], local_sem.at[0]),
         pltpu.make_async_copy(radius_ref, state.at[pl.ds(3, 1)], local_sem.at[1]),
         pltpu.make_async_copy(film_ref, state.at[pl.ds(4, 1)], local_sem.at[2]),
     ]
-    for load in loads:
+    for load in loads + flats:
         load.start()
-    greet(offsets)
+
+    def meanwhile():
+        for load in flats:
+            load.wait()
+        row = lax.broadcasted_iota(jnp.int32, (32, grains), 0)
+        for c in range(5):
+            here = (row == c) | (row == c + 8) | (row == c + 16)
+            picker[:, c * grains : (c + 1) * grains] = here.astype(jnp.float32).astype(jnp.bfloat16)
+        lax.fori_loop(0, early, own_contacts, 0)
+
+    greet(offsets, meanwhile)
     blank[...] = jnp.zeros_like(blank)
     for load in loads:
         load.wait()
@@ -123,6 +204,7 @@
         )
         fills.append(fill)
         pl.when(jnp.logical_not(present(offset)))(fill.start)
+    lax.fori_loop(early, batches, own_contacts, 0)
     inner.wait()
     for offset, copy, fill in reversed(list(zip(offsets, copies, fills))):
         pl.when(jnp.logical_not(present(offset)))(fill.wait)
@@ -176,15 +258,28 @@
     tail = place.shape[4:]
     shape = (5,) + tuple(n + 2 for n in extents) + tail
     own = pltpu.VMEM((5,) + tuple(extents) + tail, jnp.float32)
+    tiles, grains = math.prod(extents), tail[-1]
     return pl.pallas_call(
         functools.partial(spread_kernel, extents),
-        out_shape=jax.ShapeDtypeStruct(shape, jnp.float32),
-        in_specs=[anywhere] * 3,
-        out_specs=anywhere,
-        scratch_shapes=[own, own, pltpu.SemaphoreType.DMA((30,)), sems, sems],
+        out_shape=[
+            jax.ShapeDtypeStruct(shape, jnp.float32),
+            jax.ShapeDtypeStruct((3 * tiles, grains), jnp.float32),
+        ],
+        in_specs=[anywhere] * 5,
+        out_specs=[anywhere, pl.BlockSpec(memory_space=pltpu.VMEM)],
+        scratch_shapes=[
+            own,
+            own,
+            pltpu.VMEM((4 * tiles, grains), jnp.float32),
+            pltpu.VMEM((32, 5 * grains), jnp.bfloat16),
+            pltpu.SemaphoreType.DMA((30,)),
+            pltpu.SemaphoreType.DMA((2,)),
+            sems,
+            sems,
+        ],
         compiler_params=pltpu.CompilerParams(collective_id=0, has_side_effects=True),
         name="spread",
-    )(place, radius, film)
+    )(place, radius, film, place.reshape(3 * tiles, grains), radius.reshape(tiles, grains))
 
 
 def collect(totals, extents):
@@ -229,6 +324,7 @@
 def kernel(
     dims,
     border_hbm,
+    inner_ref,
     live_ref,
     partner_ref,
     rupture_ref,
@@ -251,7 +347,8 @@
     table_even,
     table_odd,
     table_more,
-    acc,
+    acc_even,
+    acc_odd,
     near,
     far,
     counts,
@@ -263,6 +360,7 @@
 ):
     bx, by, bz, grains = dims
     tables = (table_even, table_odd)
+    accs = (acc_even, acc_odd)
     wy, wz = by + 2, bz + 2
     plane = by * bz
     step = pl.program_id(0)
@@ -323,6 +421,7 @@
         near[...] = jnp.zeros_like(near)
         far[...] = jnp.zeros_like(far)
         summed[...] = jnp.zeros_like(summed)
+        acc_odd[...] = jnp.zeros_like(acc_odd)
         held[27 * plane * 8 :, :] = jnp.zeros((8, grains), f32)
         rows = lax.broadcasted_iota(jnp.int32, (grains, grains), 0)
         cols = lax.broadcasted_iota(jnp.int32, (grains, grains), 1)
@@ -505,8 +604,10 @@
         0,
         [functools.partial(scan, 1 - now)],
     )
-    for c in range(4):
-        owned[c] = sums[c]
+    for c in range(3):
+        rows = pl.ds(pl.multiple_of(c * bx * plane + step * plane, plane), plane)
+        owned[c, 8:, :] = sums[c] + inner_ref[rows, :]
+    owned[3, 8:, :] = sums[3]
     most = counts[now, plane]
 
     def distribute(group, first, into):
@@ -535,17 +636,15 @@
             part = slice(8 * block, 8 * block + 8)
             table[n, part] = jnp.broadcast_to(columns[part, c : c + 1], (8, grains))
 
-    def pushes(mine, theirs, own_tile):
-        deltas = [mine[c] - theirs[c] for c in range(3)]
-        square = deltas[0] * deltas[0] + deltas[1] * deltas[1] + deltas[2] * deltas[2]
-        if own_tile:
-            square = jnp.maximum(square, FLOOR)
-        inverse = lax.rsqrt(square)
-        inter = jnp.maximum(mine[3] + theirs[3] - square * inverse, TINY)
-        push = inter * inter * inverse * lax.rsqrt(inter * (mine[4] + theirs[4]))
-        return [push * member for member in deltas]
-
-    def contacts(local, table, groups, own_tile, beside):
+    def reduce(acc, local):
+        ones = jnp.ones((8, 2 * grains), jnp.bfloat16)
+        for c in range(3):
+            both = jnp.concatenate(split(acc[c]), axis=1)
+            value = lax.dot_general(ones, both, across, preferred_element_type=f32)
+            line = pl.ds(local + 8, 1)
+            owned[c, line, :] = owned[c, line, :] + value[0:1]
+
+    def contacts(local, table, acc, groups, beside):
         listed = [
             [
                 jnp.broadcast_to(lists[g, pl.ds(c * plane + local, 1), :], (8, grains))
@@ -553,15 +652,11 @@
             ]
             for g in groups
         ]
-        selves = [
-            jnp.broadcast_to(others[pl.ds(own_row(step * plane + local, c), 1), :], (8, grains))
-            for c in (0, 1, 2, 3, 5)
-        ]
         collected = [[jnp.zeros((8, grains), f32)] * 3 for g in groups]
         for m in range(grains // 8):
             part = slice(8 * m, 8 * m + 8)
             mine = [table[c, part] for c in range(5)]
-            both = pushes(mine, selves, True) if own_tile else None
+            both = None
             for g, theirs in enumerate(listed):
                 products = pushes(mine, theirs, False)
                 for c in range(3):
@@ -574,12 +669,6 @@
             for c in range(3):
                 line = jnp.sum(collected[g][c], axis=0, keepdims=True)
                 summed[into, pl.ds(c * plane + local, 1), :] = line
-        ones = jnp.ones((8, 2 * grains), jnp.bfloat16)
-        for c in range(3):
-            both = jnp.concatenate(split(acc[c]), axis=1)
-            value = lax.dot_general(ones, both, across, preferred_element_type=f32)
-            line = pl.ds(local, 1)
-            owned[c, line, :] = owned[c, line, :] + value[0:1]
 
     across = (((1,), (1,)), ((), ()))
     lanes = lax.broadcasted_iota(jnp.int32, (grains, grains), 0).astype(f32).astype(jnp.bfloat16)
@@ -627,6 +716,7 @@
 
     def tile_step(couple, carry):
         def run(groups):
+            reduce(acc_odd, 2 * couple - 1)
             for half in range(2):
                 local = 2 * couple + half
                 tile = step * plane + local
@@ -634,10 +724,12 @@
 
                 def beside(m):
                     spread_columns(tables[1 - half], columns, m)
-                    if m % 2 == 0:
-                        bridges(local, m // 2)
-
-                contacts(local, tables[half], groups, True, beside)
+                    if m < grains // 16:
+                        bridges(local, m)
+
+                contacts(local, tables[half], accs[half], groups, beside)
+                if half == 0:
+                    reduce(acc_even, local)
 
         crowded = jnp.maximum(counts[now, 2 * couple], counts[now, 2 * couple + 1]) > grains
 
@@ -664,6 +756,7 @@
         pltpu.make_async_copy(todo, agenda, agenda_sem).wait()
 
     lax.fori_loop(0, plane // 2, tile_step, 0)
+    reduce(acc_odd, plane - 1)
     distribute(0, 0, 0)
 
     @pl.when((most > grains) & (early > grains))
@@ -683,7 +776,8 @@
                 columns = columns_of(step * plane + local)
                 for m in range(grains // 8):
                     spread_columns(table_more, columns, m)
-                contacts(local, table_more, (0,), False, lambda m: None)
+                contacts(local, table_more, acc_even, (0,), lambda m: None)
+                reduce(acc_even, local)
 
             return inner
 
@@ -694,7 +788,7 @@
     lax.fori_loop(2, (most + grains - 1) // grains, more, 0)
     for c in range(4):
         line = far_line(step + 1, 4, c)
-        far[line, :] = far[line, :] + owned[c]
+        far[line, :] = far[line, :] + owned[c, 8:, :]
 
     @pl.when(step == pl.num_programs(0) - 1)
     def _():
@@ -722,12 +816,13 @@
     cells = (bx + 2) * (by + 2) * (bz + 2)
     extents = (bx, by, bz)
     film = film_liquid.reshape(1, bx, by, bz, 1, grains)
-    border = spread(
+    border, inner = spread(
         positions.reshape(3, bx, by, bz, 1, grains),
         grain_radii.reshape(1, bx, by, bz, 1, grains),
         film,
         extents,
-    ).reshape(5 * cells, grains)
+    )
+    border = border.reshape(5 * cells, grains)
     plane = by * bz
     span = 27 * plane
     wide = pl.BlockSpec((span, grains), lambda i: (i, 0))
@@ -739,6 +834,7 @@
             grid=(bx,),
             in_specs=[
                 pl.BlockSpec(memory_space=pl.ANY),
+                pl.BlockSpec((3 * tiles, grains), lambda i: (0, 0)),
                 pl.BlockSpec((1, slots), lambda i: (0, 0)),
                 wide,
                 wide,
@@ -758,10 +854,11 @@
                 pltpu.VMEM((2, span, grains), jnp.int32),
                 pltpu.VMEM((2, 5 * plane, grains), f32),
                 pltpu.VMEM((2, 3 * plane, grains), f32),
-                pltpu.VMEM((4, plane, grains), f32),
+                pltpu.VMEM((4, plane + 8, grains), f32),
                 pltpu.VMEM((5, grains, grains), f32),
                 pltpu.VMEM((5, grains, grains), f32),
                 pltpu.VMEM((5, grains, grains), f32),
+                pltpu.VMEM((3, grains, grains), f32),
                 pltpu.VMEM((3, grains, grains), f32),
                 pltpu.VMEM((cells * 8 + 8, grains), f32),
                 pltpu.VMEM((3 * (bx + 2) * 4 * (-(-(by + 2) * bz // 8) * 8), grains), f32),
@@ -780,6 +877,7 @@
         name="slots",
     )(
         border,
+        inner,
         pair_live.reshape(1, slots),
         partner.reshape(slots, grains),
         rupture.reshape(slots, grains),

time: 41.3 us -> 41.4 us (level); the launches traced: 41.8 us -> 40.6 us
  Pallas kernels: 41.2 us -> 39.9 us
    pallas_call x1, Pallas kernels: 22.3 us -> 19.1 us  [shards(): pl.pallas_call(functools.partial(kernel, (bx, by, bz, grains)), grid_spec...]
    pallas_call x1, Pallas kernels: 7.98 us -> 9.25 us  [collect(): pl.pallas_call(functools.partial(return_kernel, extents), out_shape=jax.S...]
    pallas_call x1, Pallas kernels: 9.42 us -> 10.1 us  [spread(): pl.pallas_call(functools.partial(spread_kernel, extents), out_shape=[jax....]
where the time goes in v1:
time: 41.4 us; the launch traced here: 40.6 us
  Pallas kernels  39.9 us (96%)
  between operations  0.65 us (2%)
    pallas_call x1, Pallas kernels, shards(): pl.pallas_call(functools.partial(kernel, (bx, by, bz, grains)), grid_spec...  19.1 us
    pallas_call x1, Pallas kernels, spread(): pl.pallas_call(functools.partial(spread_kernel, extents), out_shape=[jax....  10.1 us
    pallas_call x1, Pallas kernels, collect(): pl.pallas_call(functools.partial(return_kernel, extents), out_shape=jax.S...  9.25 us
    pallas_call x1, Pallas kernels, shards(): pl.pallas_call(finish_kernel, out_shape=[jax.ShapeDtypeStruct((3 * tiles,...  1.47 us

profile of v1, /device:TPU:0, one launch (start us, length us, event | category | flops | bytes accessed | tf_op | source)
XLA Modules:
  0.0 40.6 jit_solution(12456139043266412068)
XLA Ops:
  0.6 10.1 %spread.1 = (f32[5,6,6,4,1,128]{5,4,3,2,1,0:T(1,128)}, f32[96,128]{1,0:T(8,128)}) custom-call(f32[3,4,4,2,1,128]{5,4,3,2,1,0:T(1,128)} %bitcast.22, f32[1,4,4,2,1,128]{5,4,3,2,1,0:T(1,128)} %bitcast.24, f32[1,4,4,2,1,128]{5,4,3,2,1,0:T(1,128)} %bitcast.26, f32[96,128]{1,0:T(8,128)} %bitcast.23, f32[32,128]{1,0:T(8,128)} %bitcast.25), custom_call_target="tpu_custom_call" | custom-call | tf_op jit(solution)/shard_map/spread/pallas_call | solution.py:262
  10.7 19.1 %slots.1 = (f32[576,128]{1,0:T(8,128)}, f32[864,128]{1,0:T(8,128)}) custom-call(f32[720,128]{1,0:T(8,128)} %bitcast.19, f32[96,128]{1,0:T(8,128)} %get-tuple-element.10.inner_ref, s32[1,864]{1,0:T(1,128)} %bitcast.28, s32[864,128]{1,0:T(8,128)} %bitcast.16, s32[864,128]{1,0:T(8,128)} %bitcast.17, f32[864,128]{1,0:T(8,128)} %bitcast.18), custom_call_target="tpu_custom_call" | custom-call | tf_op jit(solution)/shard_map/slots/pallas_call | solution.py:830
  29.8 9.3 %collect.1 = f32[4,4,4,2,1,128]{5,4,3,2,1,0:T(1,128)} custom-call(f32[4,6,6,4,1,128]{5,4,3,2,1,0:T(1,128)} %bitcast.20), custom_call_target="tpu_custom_call" | custom-call | tf_op jit(solution)/shard_map/collect/pallas_call | solution.py:295
  39.1 1.5 %finish.1 = (f32[96,128]{1,0:T(8,128)}, f32[32,128]{1,0:T(8,128)}) custom-call(f32[128,128]{1,0:T(8,128)} %bitcast.21, f32[32,128]{1,0:T(8,128)} %bitcast.27), custom_call_target="tpu_custom_call" | custom-call | tf_op jit(solution)/shard_map/finish/pallas_call | solution.py:889

commit v2 on v1

--- a/solution.py
+++ b/solution.py
@@ -347,8 +347,7 @@
     table_even,
     table_odd,
     table_more,
-    acc_even,
-    acc_odd,
+    acc,
     near,
     far,
     counts,
@@ -360,7 +359,6 @@
 ):
     bx, by, bz, grains = dims
     tables = (table_even, table_odd)
-    accs = (acc_even, acc_odd)
     wy, wz = by + 2, bz + 2
     plane = by * bz
     step = pl.program_id(0)
@@ -421,12 +419,13 @@
         near[...] = jnp.zeros_like(near)
         far[...] = jnp.zeros_like(far)
         summed[...] = jnp.zeros_like(summed)
-        acc_odd[...] = jnp.zeros_like(acc_odd)
         held[27 * plane * 8 :, :] = jnp.zeros((8, grains), f32)
         rows = lax.broadcasted_iota(jnp.int32, (grains, grains), 0)
         cols = lax.broadcasted_iota(jnp.int32, (grains, grains), 1)
         half = grains // 2
-        for n, last in enumerate((cols, grains, half - 1, half // 2 - 1, half + half // 2 - 1)):
+        marks = [half - 1, half // 2 - 1, half + half // 2 - 1]
+        marks += [(2 * n + 1) * grains // 8 - 1 for n in range(4)]
+        for n, last in enumerate([cols, grains] + marks):
             block = (rows <= last).astype(f32).astype(jnp.bfloat16)
             triangle[:, n * grains : (n + 1) * grains] = block
         flags[...] = jnp.zeros_like(flags)
@@ -502,7 +501,7 @@
             part = slice(s * plane, (s + 1) * plane)
             ahead = prefix[part, 0:grains]
             before[slot, part, :] = ahead
-            for n in range(3):
+            for n in range(7):
                 probes[slot, n, part, :] = prefix[part, (n + 2) * grains : (n + 3) * grains]
             offset[slot, i * plane : (i + 1) * plane, :] = total
             spot = jnp.where(mask[part, :] > 0.0, total + ahead - 1.0, -1.0)
@@ -522,20 +521,24 @@
         wanted = (lane + group * grains).astype(f32)
         half = grains // 2
         index = {}
-        bit = half // 2
+        bit = grains // 8
         level = 0
         while bit:
             for i, s in list(enumerate(outer))[first:]:
                 part = slice(s * plane, (s + 1) * plane)
                 rank = wanted - offset[now, i * plane : (i + 1) * plane, :]
-                if bit == half // 2:
-                    upper = probes[now, 0, part, :] <= rank
-                    probe = jnp.where(upper, probes[now, 2, part, :], probes[now, 1, part, :])
-                    index[s] = jnp.where(upper, half, 0)
+                if bit == grains // 8:
+                    marks = [probes[now, n, part, :] for n in range(7)]
+                    upper = marks[0] <= rank
+                    second = jnp.where(upper, marks[2], marks[1]) <= rank
+                    high = jnp.where(second, marks[6], marks[5])
+                    low = jnp.where(second, marks[4], marks[3])
+                    probe = jnp.where(upper, high, low)
+                    index[s] = jnp.where(upper, half, 0) + jnp.where(second, half // 2, 0)
                 else:
                     probe = take(before[now, part, :], index[s] + (bit - 1))
                 index[s] = jnp.where(probe <= rank, index[s] + bit, index[s])
-            for work in beside[level::6]:
+            for work in beside[level::5]:
                 work()
             bit //= 2
             level += 1
@@ -606,8 +609,8 @@
     )
     for c in range(3):
         rows = pl.ds(pl.multiple_of(c * bx * plane + step * plane, plane), plane)
-        owned[c, 8:, :] = sums[c] + inner_ref[rows, :]
-    owned[3, 8:, :] = sums[3]
+        owned[c] = sums[c] + inner_ref[rows, :]
+    owned[3] = sums[3]
     most = counts[now, plane]
 
     def distribute(group, first, into):
@@ -636,15 +639,7 @@
             part = slice(8 * block, 8 * block + 8)
             table[n, part] = jnp.broadcast_to(columns[part, c : c + 1], (8, grains))
 
-    def reduce(acc, local):
-        ones = jnp.ones((8, 2 * grains), jnp.bfloat16)
-        for c in range(3):
-            both = jnp.concatenate(split(acc[c]), axis=1)
-            value = lax.dot_general(ones, both, across, preferred_element_type=f32)
-            line = pl.ds(local + 8, 1)
-            owned[c, line, :] = owned[c, line, :] + value[0:1]
-
-    def contacts(local, table, acc, groups, beside):
+    def contacts(local, table, groups, beside):
         listed = [
             [
                 jnp.broadcast_to(lists[g, pl.ds(c * plane + local, 1), :], (8, grains))
@@ -669,6 +664,12 @@
             for c in range(3):
                 line = jnp.sum(collected[g][c], axis=0, keepdims=True)
                 summed[into, pl.ds(c * plane + local, 1), :] = line
+        ones = jnp.ones((8, 2 * grains), jnp.bfloat16)
+        for c in range(3):
+            both = jnp.concatenate(split(acc[c]), axis=1)
+            value = lax.dot_general(ones, both, across, preferred_element_type=f32)
+            line = pl.ds(local, 1)
+            owned[c, line, :] = owned[c, line, :] + value[0:1]
 
     across = (((1,), (1,)), ((), ()))
     lanes = lax.broadcasted_iota(jnp.int32, (grains, grains), 0).astype(f32).astype(jnp.bfloat16)
@@ -716,7 +717,6 @@
 
     def tile_step(couple, carry):
         def run(groups):
-            reduce(acc_odd, 2 * couple - 1)
             for half in range(2):
                 local = 2 * couple + half
                 tile = step * plane + local
@@ -724,12 +724,10 @@
 
                 def beside(m):
                     spread_columns(tables[1 - half], columns, m)
-                    if m < grains // 16:
-                        bridges(local, m)
-
-                contacts(local, tables[half], accs[half], groups, beside)
-                if half == 0:
-                    reduce(acc_even, local)
+                    if m % 2 == 0:
+                        bridges(local, m // 2)
+
+                contacts(local, tables[half], groups, beside)
 
         crowded = jnp.maximum(counts[now, 2 * couple], counts[now, 2 * couple + 1]) > grains
 
@@ -756,7 +754,6 @@
         pltpu.make_async_copy(todo, agenda, agenda_sem).wait()
 
     lax.fori_loop(0, plane // 2, tile_step, 0)
-    reduce(acc_odd, plane - 1)
     distribute(0, 0, 0)
 
     @pl.when((most > grains) & (early > grains))
@@ -776,8 +773,7 @@
                 columns = columns_of(step * plane + local)
                 for m in range(grains // 8):
                     spread_columns(table_more, columns, m)
-                contacts(local, table_more, acc_even, (0,), lambda m: None)
-                reduce(acc_even, local)
+                contacts(local, table_more, (0,), lambda m: None)
 
             return inner
 
@@ -788,7 +784,7 @@
     lax.fori_loop(2, (most + grains - 1) // grains, more, 0)
     for c in range(4):
         line = far_line(step + 1, 4, c)
-        far[line, :] = far[line, :] + owned[c, 8:, :]
+        far[line, :] = far[line, :] + owned[c]
 
     @pl.when(step == pl.num_programs(0) - 1)
     def _():
@@ -845,20 +841,19 @@
                 pltpu.VMEM(((bx + 2) * 9 * 6 * plane, grains), f32),
                 pltpu.VMEM((tiles, grains), f32),
                 pltpu.VMEM((slots, grains), f32),
-                pltpu.VMEM((grains, 5 * grains), jnp.bfloat16),
+                pltpu.VMEM((grains, 9 * grains), jnp.bfloat16),
                 pltpu.VMEM((span * 8 + 8, grains), f32),
                 pltpu.VMEM((span, grains), f32),
                 pltpu.VMEM((2, span, grains), f32),
-                pltpu.VMEM((2, 3, span, grains), f32),
+                pltpu.VMEM((2, 7, span, grains), f32),
                 pltpu.VMEM((2, span + plane, grains), f32),
                 pltpu.VMEM((2, span, grains), jnp.int32),
                 pltpu.VMEM((2, 5 * plane, grains), f32),
                 pltpu.VMEM((2, 3 * plane, grains), f32),
-                pltpu.VMEM((4, plane + 8, grains), f32),
+                pltpu.VMEM((4, plane, grains), f32),
                 pltpu.VMEM((5, grains, grains), f32),
                 pltpu.VMEM((5, grains, grains), f32),
                 pltpu.VMEM((5, grains, grains), f32),
-                pltpu.VMEM((3, grains, grains), f32),
                 pltpu.VMEM((3, grains, grains), f32),
                 pltpu.VMEM((cells * 8 + 8, grains), f32),
                 pltpu.VMEM((3 * (bx + 2) * 4 * (-(-(by + 2) * bz // 8) * 8), grains), f32),

time: 41.4 us -> 41.2 us (level); the launches traced: 40.6 us -> 41.1 us
  Pallas kernels: 39.9 us -> 40.5 us
    pallas_call x1, Pallas kernels: 9.25 us -> 9.76 us  [collect(): pl.pallas_call(functools.partial(return_kernel, extents), out_shape=jax.S...]
where the time goes in v2:
time: 41.2 us; the launch traced here: 41.1 us
  Pallas kernels  40.5 us (98%)
  between operations  0.65 us (2%)
    pallas_call x1, Pallas kernels, shards(): pl.pallas_call(functools.partial(kernel, (bx, by, bz, grains)), grid_spec...  19.2 us
    pallas_call x1, Pallas kernels, spread(): pl.pallas_call(functools.partial(spread_kernel, extents), out_shape=[jax....  10.1 us
    pallas_call x1, Pallas kernels, collect(): pl.pallas_call(functools.partial(return_kernel, extents), out_shape=jax.S...  9.76 us
    pallas_call x1, Pallas kernels, shards(): pl.pallas_call(finish_kernel, out_shape=[jax.ShapeDtypeStruct((3 * tiles,...  1.47 us

profile of v2, /device:TPU:0, one launch (start us, length us, event | category | flops | bytes accessed | tf_op | source)
XLA Modules:
  0.0 41.1 jit_solution(2383016446307220936)
XLA Ops:
  0.6 10.1 %spread.1 = (f32[5,6,6,4,1,128]{5,4,3,2,1,0:T(1,128)}, f32[96,128]{1,0:T(8,128)}) custom-call(f32[3,4,4,2,1,128]{5,4,3,2,1,0:T(1,128)} %bitcast.22, f32[1,4,4,2,1,128]{5,4,3,2,1,0:T(1,128)} %bitcast.24, f32[1,4,4,2,1,128]{5,4,3,2,1,0:T(1,128)} %bitcast.26, f32[96,128]{1,0:T(8,128)} %bitcast.23, f32[32,128]{1,0:T(8,128)} %bitcast.25), custom_call_target="tpu_custom_call" | custom-call | tf_op jit(solution)/shard_map/spread/pallas_call | solution.py:262
  10.7 19.2 %slots.1 = (f32[576,128]{1,0:T(8,128)}, f32[864,128]{1,0:T(8,128)}) custom-call(f32[720,128]{1,0:T(8,128)} %bitcast.19, f32[96,128]{1,0:T(8,128)} %get-tuple-element.10.inner_ref, s32[1,864]{1,0:T(1,128)} %bitcast.28, s32[864,128]{1,0:T(8,128)} %bitcast.16, s32[864,128]{1,0:T(8,128)} %bitcast.17, f32[864,128]{1,0:T(8,128)} %bitcast.18), custom_call_target="tpu_custom_call" | custom-call | tf_op jit(solution)/shard_map/slots/pallas_call | solution.py:826
  29.9 9.8 %collect.1 = f32[4,4,4,2,1,128]{5,4,3,2,1,0:T(1,128)} custom-call(f32[4,6,6,4,1,128]{5,4,3,2,1,0:T(1,128)} %bitcast.20), custom_call_target="tpu_custom_call" | custom-call | tf_op jit(solution)/shard_map/collect/pallas_call | solution.py:295
  39.7 1.5 %finish.1 = (f32[96,128]{1,0:T(8,128)}, f32[32,128]{1,0:T(8,128)}) custom-call(f32[128,128]{1,0:T(8,128)} %bitcast.21, f32[32,128]{1,0:T(8,128)} %bitcast.27), custom_call_target="tpu_custom_call" | custom-call | tf_op jit(solution)/shard_map/finish/pallas_call | solution.py:884
